TPU v7x, 32 devices: a whole 2x2x4 slice. The times are simulated.
32 devices in a mesh: gx: 8 (over y, x, core), gy: 4 (over z).
Axes of the slice: x: 2, y: 2, z: 4, core: 2. Of those that a mesh axis runs over, the one named last changes fastest.
Arguments:
- grad_p: float32 [3, 128, 64, 128], P(None, 'gx', 'gy'), may hold values from -6 to 6
- grad_s: float32 [3, 128, 64, 128], P(None, 'gx', 'gy'), may hold values from -6 to 6
- acc_p: float32 [128, 64, 128], P('gx', 'gy'), may hold values from 0.2 to 2
- acc_s: float32 [128, 64, 128], P('gx', 'gy'), may hold values from 0.2 to 2
- trans_x: float32 [128, 64, 128], P('gx', 'gy'), may hold values from 0.1 to 10
- trans_y: float32 [128, 64, 128], P('gx', 'gy'), may hold values from 0.1 to 10
- trans_z: float32 [128, 64, 128], P('gx', 'gy'), may hold values from 0.1 to 10
- c_pp: float32 [3, 128, 64, 128], P(None, 'gx', 'gy'), may hold values from 0.05 to 0.5
- c_ss: float32 [3, 128, 64, 128], P(None, 'gx', 'gy'), may hold values from 0.2 to 2
- c_ps: float32 [3, 128, 64, 128], P(None, 'gx', 'gy'), may hold values from -0.2 to 0.2
- c_sp: float32 [3, 128, 64, 128], P(None, 'gx', 'gy'), may hold values from -0.5 to 0.5
- frac: float32 [3, 128, 64, 128], P(None, 'gx', 'gy'), may hold values from 0 to 0.5
- mobility: float32 [3, 128, 64, 128], P(None, 'gx', 'gy'), may hold values from 0.5 to 2
- rate_mis: float32 [64, 3], P(('gx', 'gy')), may hold values from -6 to 6
- bhp_mis: float32 [64, 3], P(('gx', 'gy')), may hold values from -6 to 6
- control: int32 [64, 3], P(('gx', 'gy')), may hold values from 0 to 1
- perf_well: int32 [4096], P(('gx', 'gy')), may hold values from 0 to 63
- perf_cell: int32 [4096], P(('gx', 'gy')), may hold values from 0 to 32767
- perf_wi: float32 [4096], P(('gx', 'gy')), may hold values from 1 to 10
Outputs:
- lam_p: float32 [128, 64, 128], P('gx', 'gy')
- lam_s: float32 [128, 64, 128], P('gx', 'gy')
- well_grad: float32 [64, 3], P(('gx', 'gy'))
Inputs may be any that keep to these rules, and one draw needn't show every extreme that they name: perf_cell indexes the block of the device that holds the slot, as (i * 16 + j) * 128 + k; slots may share a cell. `perf_well`: well w is held by the device of flat index w // 2 along gx+gy; a well's slots may lie on any devices.
All inputs are finite; a program needn't handle non-finite values.
Results may differ from a plain program's by a relative error of at most 0.0002.
Values sent between devices are 32-bit elements; how exact they have to be, the bound alone decides.
No kernel may reach another device: no remote copies, remote signals or barrier semaphores. Data moves between devices by JAX's collectives and lax.ppermute only.
A program may use at most 128 MiB of HBM per device.

v0:
```python
import jax
import jax.numpy as jnp
from jax import lax
from jax.sharding import PartitionSpec as P

SWEEPS = 8
omega_factor = 0.8


def passed_along(value, axis, by):
    length = lax.axis_size(axis)
    pairs = [(i, i + by) for i in range(length) if 0 <= i + by < length]
    return lax.ppermute(value, axis, pairs)


def padded_2(block, sides, width):
    for axis, dim in sides:
        count = lax.axis_size(axis)
        forward = [(i, i + 1) for i in range(count - 1)]
        backward = [(target, source) for source, target in forward]
        low = lax.ppermute(
            lax.slice_in_dim(block, block.shape[dim] - width, None, axis=dim), axis, forward
        )
        high = lax.ppermute(lax.slice_in_dim(block, 0, width, axis=dim), axis, backward)
        block = jnp.concatenate([low, block, high], axis=dim)
    return block


def neighbour_sum(fields, table):
    centre = fields[:, 1:-1, 1:-1, :]
    east = fields[:, 2:, 1:-1, :]
    west = fields[:, :-2, 1:-1, :]
    north = fields[:, 1:-1, 2:, :]
    south = fields[:, 1:-1, :-2, :]
    upper = jnp.pad(centre[..., 1:], ((0, 0), (0, 0), (0, 0), (0, 1)))
    lower = jnp.pad(centre[..., :-1], ((0, 0), (0, 0), (0, 0), (1, 0)))
    total = table[8] * east + table[9] * west
    total = total + table[10] * north + table[11] * south
    total = total + table[12] * upper + table[13] * lower
    return (centre, total)


def relax(fields, table):
    centre, beside_all = neighbour_sum(fields, table)
    weight_sum = table[14]
    laplace = weight_sum * centre - beside_all
    old_a = centre[0]
    old_b = centre[1]
    out_a = table[0] * old_a + laplace[0] + table[3] * old_b + table[4] * laplace[1]
    out_b = table[2] * old_a + table[1] * old_b + table[5] * laplace[1]
    new_a = old_a + table[15] * (table[6] - out_a)
    new_b = old_b + table[16] * (table[7] - out_b)
    return jnp.stack([new_a, new_b])


def local(
    grad_p,
    grad_s,
    acc_p,
    acc_s,
    trans_x,
    trans_y,
    trans_z,
    c_pp,
    c_ss,
    c_ps,
    c_sp,
    frac,
    mobility,
    rate_mis,
    bhp_mis,
    control,
    perf_well,
    perf_cell,
    perf_wi,
):
    rows_x, rows_y, layers = trans_x.shape
    steps = grad_p.shape[0]
    sweeps = SWEEPS
    cells = rows_x * rows_y * layers
    gx_at = lax.axis_index("gx")
    gy_at = lax.axis_index("gy")
    east_plane = passed_along(trans_x[0:1], "gx", -1)
    north_plane = passed_along(trans_y[:, 0:1], "gy", -1)
    first_x = lax.broadcasted_iota(jnp.int32, (rows_x, 1, 1), 0) + gx_at * rows_x > 0
    first_y = lax.broadcasted_iota(jnp.int32, (1, rows_y, 1), 1) + gy_at * rows_y > 0
    first_z = lax.broadcasted_iota(jnp.int32, (1, 1, layers), 2) > 0
    w_east = jnp.concatenate([trans_x[1:], east_plane], axis=0)
    w_west = jnp.where(first_x, trans_x, 0.0)
    w_north = jnp.concatenate([trans_y[:, 1:], north_plane], axis=1)
    w_south = jnp.where(first_y, trans_y, 0.0)
    w_up = jnp.pad(trans_z[:, :, 1:], ((0, 0), (0, 0), (0, 1)))
    w_down = jnp.where(first_z, trans_z, 0.0)
    weight_sum = w_east + w_west + w_north + w_south + w_up + w_down
    effective = jnp.where(control == 1, rate_mis, bhp_mis)
    all_rows = lax.all_gather(effective, ("gx", "gy"), axis=0, tiled=True)
    well_count = all_rows.shape[0]
    selector = (perf_well[:, None] == jnp.arange(well_count, dtype=jnp.int32)[None, :]).astype(
        jnp.float32
    )
    perf_rows = jnp.dot(selector, all_rows, precision=lax.Precision.HIGHEST)
    sources = (
        jnp.zeros((steps, cells), jnp.float32)
        .at[:, perf_cell]
        .add((perf_wi[:, None] * perf_rows).T)
    )
    sources = sources.reshape(steps, rows_x, rows_y, layers)
    multipliers = jnp.zeros((2, rows_x, rows_y, layers), jnp.float32)
    returned = [None] * steps
    for step_index in reversed(range(steps)):
        right_a = grad_p[step_index] + sources[step_index] + acc_p * multipliers[0]
        right_b = grad_s[step_index] + acc_s * multipliers[1]
        scale_a = omega_factor / (c_pp[step_index] + weight_sum)
        scale_b = omega_factor / (c_ss[step_index] + mobility[step_index] * weight_sum)
        table = jnp.stack(
            [
                c_pp[step_index],
                c_ss[step_index],
                c_ps[step_index],
                c_sp[step_index],
                frac[step_index],
                mobility[step_index],
                right_a,
                right_b,
                w_east,
                w_west,
                w_north,
                w_south,
                w_up,
                w_down,
                weight_sum,
                scale_a,
                scale_b,
            ]
        )
        for sweep_index in range(sweeps):
            padded = padded_2(multipliers, (("gx", 1), ("gy", 2)), 1)
            multipliers = relax(padded, table)
        flat_fields = multipliers.reshape(2, cells)
        at_cells = flat_fields[:, perf_cell]
        at_frac = frac[step_index].reshape(cells)[perf_cell]
        returned[step_index] = perf_wi * (at_cells[0] + at_frac * at_cells[1])
    contributions = jnp.stack(returned, axis=1)
    dense = jnp.dot(selector.T, contributions, precision=lax.Precision.HIGHEST)
    well_grad = lax.psum_scatter(dense, ("gx", "gy"), scatter_dimension=0, tiled=True)
    return (multipliers[0], multipliers[1], well_grad)


def solution(mesh):
    placed = (
        P(None, "gx", "gy", None),
        P(None, "gx", "gy", None),
        P("gx", "gy", None),
        P("gx", "gy", None),
        P("gx", "gy", None),
        P("gx", "gy", None),
        P("gx", "gy", None),
        P(None, "gx", "gy", None),
        P(None, "gx", "gy", None),
        P(None, "gx", "gy", None),
        P(None, "gx", "gy", None),
        P(None, "gx", "gy", None),
        P(None, "gx", "gy", None),
        P(("gx", "gy"), None),
        P(("gx", "gy"), None),
        P(("gx", "gy"), None),
        P(("gx", "gy")),
        P(("gx", "gy")),
        P(("gx", "gy")),
    )
    return jax.shard_map(
        local,
        mesh=mesh,
        in_specs=placed,
        out_specs=(P("gx", "gy", None), P("gx", "gy", None), P(("gx", "gy"), None)),
        check_vma=False,
    )
```

profile of v0, /device:TPU:0, one launch (start us, length us, event | category | flops | bytes accessed | tf_op | source)
XLA Modules:
  0.0 621.0 jit_solution(6534651151224634101)
XLA Ops:
  10.5 71.9 %all-gather = f32[32,2,3]{2,1,0:T(2,128)S(1)} all-gather(f32[1,2,3]{2,1,0:T(2,128)S(1)} %fusion.643), channel_id=1, replica_groups=mesh['gx'=8,'gy'=4] {'gx','gy'}, dimensions={0}, use_global_device_ids=true | all-gather | bytes 792 | tf_op jit(solution)/shard_map/all_gather | solution.py:96
  83.4 7.8 %scatter_custom_fusion = f32[3,32768]{0,1:T(8,128)} fusion(s32[128]{0:T(128)S(1)} %compare_select_fusion, f32[128,3]{1,0:T(8,128)S(1)} %copy.30, f32[]{:T(128)} %constant.14.clone.1), kind=kCustom, calls=%fused_computation.10 | custom fusion | flops 384 | bytes 393220 | tf_op jit(solution)/shard_map/scatter-add | solution.py:105
  91.4 30.5 %slice_reduce_fusion = (f32[32768]{0:T(1024)S(1)}, f32[32768]{0:T(1024)S(1)}, f32[32768]{0:T(1024)S(1)}) fusion(f32[3,32768]{0,1:T(8,128)} %scatter_custom_fusion), kind=kLoop, calls=%fused_computation.7 | loop fusion | bytes 786432 | tf_op jit(solution)/shard_map/slice | solution.py:111
  123.6 4.5 collective-permute-start.5
  136.6 4.8 collective-permute-start.9
  149.7 4.8 collective-permute-start.13
  164.7 4.5 collective-permute-start.17
  173.6 5.1 collective-permute-start.19
  180.9 4.7 collective-permute-start.21
  189.8 5.1 collective-permute-start.23
  197.1 4.5 collective-permute-start.25
  205.9 5.1 collective-permute-start.27
  213.2 4.5 collective-permute-start.29
  222.1 5.1 collective-permute-start.31
  229.4 4.5 collective-permute-start.33
  238.3 6.0 collective-permute-start.35
  246.5 4.5 collective-permute-start.37
  254.3 6.0 collective-permute-start.39
  262.5 4.5 collective-permute-start.41
  270.2 6.0 collective-permute-start.43
  278.4 4.5 collective-permute-start.45
  287.3 6.0 collective-permute-start.47
  295.5 4.5 collective-permute-start.49
  304.3 6.0 collective-permute-start.51
  312.5 4.5 collective-permute-start.53
  321.4 6.0 collective-permute-start.55
  338.5 6.0 collective-permute-start.59
  355.6 6.0 collective-permute-start.63
  363.8 4.5 collective-permute-start.65
  372.7 6.0 collective-permute-start.67
  380.9 4.5 collective-permute-start.69
  388.7 6.0 collective-permute-start.71
  404.6 6.0 collective-permute-start.75
  412.8 4.5 collective-permute-start.77
  421.7 6.6 %collective-permute-start.79 = (f32[2,1,16,128]{3,2,1,0:T(8,128)}, f32[2,1,16,128]{3,2,1,0:T(8,128)}, u32[]{:S(2)}, u32[]{:S(2)}) collective-permute-start(f32[2,1,16,128]{3,2,1,0:T(8,128)} %get-tuple-element.147), channel_id=1, source_target_pairs={{0,4},{4,8},{8,12},{12,16},{16,20},{20,24},{24,28},{1,5},{5,9},{9,... | collective-permute-start | bytes 49160 | tf_op jit(solution)/shard_map/ppermute | solution.py:21
  438.7 4.5 collective-permute-start.81
  450.2 6.6 %collective-permute-start.83 = (f32[2,1,16,128]{3,2,1,0:T(8,128)}, f32[2,1,16,128]{3,2,1,0:T(8,128)}, u32[]{:S(2)}, u32[]{:S(2)}) collective-permute-start(f32[2,1,16,128]{3,2,1,0:T(8,128)} %get-tuple-element.143), channel_id=1, source_target_pairs={{0,4},{4,8},{8,12},{12,16},{16,20},{20,24},{24,28},{1,5},{5,9},{9,... | collective-permute-start | bytes 49160 | tf_op jit(solution)/shard_map/ppermute | solution.py:21
  458.7 8.9 %copy.33 = f32[2,32768]{0,1:T(8,128)} copy(f32[2,32768]{1,0:T(2,128)} %pad_maximum_fusion.307) | data formatting | bytes 524288 | tf_op jit(solution)/shard_map/stack | solution.py:53
  467.6 7.1 %gather_fusion.4 = f32[128,2]{1,0:T(8,128)} fusion(f32[2,32768]{0,1:T(8,128)} %copy.33, s32[1024]{0:T(1024)} %pad_clamp_fusion), kind=kCustom, calls=%fused_computation.4 | custom fusion | bytes 2560 | tf_op jit(solution)/shard_map/gather | solution.py:140
  477.0 4.5 collective-permute-start.85
  487.3 5.5 collective-permute-start.87
  495.8 4.6 collective-permute-start.89
  505.7 6.6 %collective-permute-start.91 = (f32[2,1,16,128]{3,2,1,0:T(8,128)}, f32[2,1,16,128]{3,2,1,0:T(8,128)}, u32[]{:S(2)}, u32[]{:S(2)}) collective-permute-start(f32[2,1,16,128]{3,2,1,0:T(8,128)} %get-tuple-element.135), channel_id=1, source_target_pairs={{0,4},{4,8},{8,12},{12,16},{16,20},{20,24},{24,28},{1,5},{5,9},{9,... | collective-permute-start | bytes 49160 | tf_op jit(solution)/shard_map/ppermute | solution.py:21
  514.2 8.9 %copy.32 = f32[2,32768]{0,1:T(8,128)} copy(f32[2,32768]{1,0:T(2,128)} %pad_maximum_fusion.306) | data formatting | bytes 524288 | tf_op jit(solution)/shard_map/stack | solution.py:53
  523.1 7.1 %gather_fusion.2 = f32[128,2]{1,0:T(8,128)} fusion(f32[2,32768]{0,1:T(8,128)} %copy.32, s32[1024]{0:T(1024)} %pad_clamp_fusion), kind=kCustom, calls=%fused_computation.2 | custom fusion | bytes 2560 | tf_op jit(solution)/shard_map/gather | solution.py:140
  557.4 8.4 %copy.31 = f32[2,32768]{0,1:T(8,128)} copy(f32[2,32768]{1,0:T(2,128)S(1)} %pad_maximum_fusion.305) | data formatting | bytes 524288 | tf_op jit(solution)/shard_map/stack | solution.py:53
  565.8 6.5 %gather_fusion = f32[128,2]{1,0:T(8,128)S(1)} fusion(f32[2,32768]{0,1:T(8,128)} %copy.31, s32[1024]{0:T(1024)} %pad_clamp_fusion), kind=kCustom, calls=%fused_computation | custom fusion | bytes 2560 | tf_op jit(solution)/shard_map/gather | solution.py:140
  572.9 47.6 %all-reduce.51 = f32[64,3]{1,0:T(8,128)S(1)} all-reduce(f32[64,3]{1,0:T(8,128)S(1)} %fusion.588), channel_id=2, replica_groups=mesh['gx'=8,'gy'=4] {'gx','gy'}, use_global_device_ids=true, to_apply=%region_1.2.clone | all-reduce | flops 192 | bytes 1536
  (382 shorter events, 213.9 us)
Async XLA Ops:
  0.6 121.5 %collective-permute-start.2 = (f32[2,1,16,128]{3,2,1,0:T(8,128)S(1)}, f32[2,1,16,128]{3,2,1,0:T(8,128)S(1)}, u32[]{:S(2)}, u32[]{:S(2)}) collective-permute-start(f32[2,1,16,128]{3,2,1,0:T(8,128)S(1)} %broadcast.163), channel_id=1, source_target_pairs={{4,0},{8,4},{12,8},{16,12},{20,16},{24,20},{28,24},{5,1},{9,5},{13... | collective-permute-start | bytes 49160 | tf_op jit(solution)/shard_map/ppermute | solution.py:24
  1.9 120.2 %collective-permute-start.3 = (f32[2,1,16,128]{3,2,1,0:T(8,128)S(1)}, f32[2,1,16,128]{3,2,1,0:T(8,128)S(1)}, u32[]{:S(2)}, u32[]{:S(2)}) collective-permute-start(f32[2,1,16,128]{3,2,1,0:T(8,128)S(1)} %broadcast.163), channel_id=1, source_target_pairs={{0,4},{4,8},{8,12},{12,16},{16,20},{20,24},{24,28},{1,5},{5,9},{9,... | collective-permute-start | bytes 49160 | tf_op jit(solution)/shard_map/ppermute | solution.py:21
  5.7 116.3 %collective-permute-start = (f32[1,16,128]{2,1,0:T(8,128)S(1)}, f32[1,16,128]{2,1,0:T(8,128)S(1)}, u32[]{:S(2)}, u32[]{:S(2)}) collective-permute-start(f32[1,16,128]{2,1,0:T(8,128)S(1)} %slice.1103), channel_id=1, source_target_pairs={{4,0},{8,4},{12,8},{16,12},{20,16},{24,20},{28,24},{5,1},{9,5},{13... | collective-permute-start | bytes 24584 | tf_op jit(solution)/shard_map/ppermute | solution.py:13
  7.8 114.2 %collective-permute-start.1 = (f32[16,1,128]{2,1,0:T(1,128)S(1)}, f32[16,1,128]{2,1,0:T(1,128)S(1)}, u32[]{:S(2)}, u32[]{:S(2)}) collective-permute-start(f32[16,1,128]{2,1,0:T(1,128)S(1)} %slice.1105), channel_id=1, source_target_pairs={{1,0},{2,1},{3,2},{5,4},{6,5},{7,6},{9,8},{10,9},{11,10},{13,12},{... | collective-permute-start | bytes 24584 | tf_op jit(solution)/shard_map/ppermute | solution.py:13
  135.3 6.3 %collective-permute-start.8 = (f32[2,18,1,128]{3,2,1,0:T(1,128)S(1)}, f32[2,18,1,128]{3,2,1,0:T(1,128)S(1)}, u32[]{:S(2)}, u32[]{:S(2)}) collective-permute-start(f32[2,18,1,128]{3,2,1,0:T(1,128)S(1)} %get-tuple-element.125), channel_id=1, source_target_pairs={{1,0},{2,1},{3,2},{5,4},{6,5},{7,6},{9,8},{10,9},{11,10},{13,12},{... | collective-permute-start | bytes 55304 | tf_op jit(solution)/shard_map/ppermute | solution.py:24
  136.6 6.3 %collective-permute-start.9 = (f32[2,18,1,128]{3,2,1,0:T(1,128)S(1)}, f32[2,18,1,128]{3,2,1,0:T(1,128)S(1)}, u32[]{:S(2)}, u32[]{:S(2)}) collective-permute-start(f32[2,18,1,128]{3,2,1,0:T(1,128)S(1)} %get-tuple-element.126), channel_id=1, source_target_pairs={{0,1},{1,2},{2,3},{4,5},{5,6},{6,7},{8,9},{9,10},{10,11},{12,13},{... | collective-permute-start | bytes 55304 | tf_op jit(solution)/shard_map/ppermute | solution.py:21
  148.4 6.3 %collective-permute-start.12 = (f32[2,18,1,128]{3,2,1,0:T(1,128)S(1)}, f32[2,18,1,128]{3,2,1,0:T(1,128)S(1)}, u32[]{:S(2)}, u32[]{:S(2)}) collective-permute-start(f32[2,18,1,128]{3,2,1,0:T(1,128)S(1)} %get-tuple-element.123), channel_id=1, source_target_pairs={{1,0},{2,1},{3,2},{5,4},{6,5},{7,6},{9,8},{10,9},{11,10},{13,12},{... | collective-permute-start | bytes 55304 | tf_op jit(solution)/shard_map/ppermute | solution.py:24
  149.7 6.3 %collective-permute-start.13 = (f32[2,18,1,128]{3,2,1,0:T(1,128)S(1)}, f32[2,18,1,128]{3,2,1,0:T(1,128)S(1)}, u32[]{:S(2)}, u32[]{:S(2)}) collective-permute-start(f32[2,18,1,128]{3,2,1,0:T(1,128)S(1)} %get-tuple-element.124), channel_id=1, source_target_pairs={{0,1},{1,2},{2,3},{4,5},{5,6},{6,7},{8,9},{9,10},{10,11},{12,13},{... | collective-permute-start | bytes 55304 | tf_op jit(solution)/shard_map/ppermute | solution.py:21
  172.3 6.5 %collective-permute-start.18 = (f32[2,1,16,128]{3,2,1,0:T(8,128)S(1)}, f32[2,1,16,128]{3,2,1,0:T(8,128)S(1)}, u32[]{:S(2)}, u32[]{:S(2)}) collective-permute-start(f32[2,1,16,128]{3,2,1,0:T(8,128)S(1)} %get-tuple-element.208), channel_id=1, source_target_pairs={{4,0},{8,4},{12,8},{16,12},{20,16},{24,20},{28,24},{5,1},{9,5},{13... | collective-permute-start | bytes 49160 | tf_op jit(solution)/shard_map/ppermute | solution.py:24
  179.6 6.2 collective-permute-start.20
  188.5 6.5 %collective-permute-start.22 = (f32[2,1,16,128]{3,2,1,0:T(8,128)S(1)}, f32[2,1,16,128]{3,2,1,0:T(8,128)S(1)}, u32[]{:S(2)}, u32[]{:S(2)}) collective-permute-start(f32[2,1,16,128]{3,2,1,0:T(8,128)S(1)} %get-tuple-element.204), channel_id=1, source_target_pairs={{4,0},{8,4},{12,8},{16,12},{20,16},{24,20},{28,24},{5,1},{9,5},{13... | collective-permute-start | bytes 49160 | tf_op jit(solution)/shard_map/ppermute | solution.py:24
  204.6 6.5 %collective-permute-start.26 = (f32[2,1,16,128]{3,2,1,0:T(8,128)S(1)}, f32[2,1,16,128]{3,2,1,0:T(8,128)S(1)}, u32[]{:S(2)}, u32[]{:S(2)}) collective-permute-start(f32[2,1,16,128]{3,2,1,0:T(8,128)S(1)} %get-tuple-element.200), channel_id=1, source_target_pairs={{4,0},{8,4},{12,8},{16,12},{20,16},{24,20},{28,24},{5,1},{9,5},{13... | collective-permute-start | bytes 49160 | tf_op jit(solution)/shard_map/ppermute | solution.py:24
  220.8 6.5 %collective-permute-start.30 = (f32[2,1,16,128]{3,2,1,0:T(8,128)S(1)}, f32[2,1,16,128]{3,2,1,0:T(8,128)S(1)}, u32[]{:S(2)}, u32[]{:S(2)}) collective-permute-start(f32[2,1,16,128]{3,2,1,0:T(8,128)S(1)} %get-tuple-element.196), channel_id=1, source_target_pairs={{4,0},{8,4},{12,8},{16,12},{20,16},{24,20},{28,24},{5,1},{9,5},{13... | collective-permute-start | bytes 49160 | tf_op jit(solution)/shard_map/ppermute | solution.py:24
  237.0 7.4 %collective-permute-start.34 = (f32[2,1,16,128]{3,2,1,0:T(8,128)S(1)}, f32[2,1,16,128]{3,2,1,0:T(8,128)S(1)}, u32[]{:S(2)}, u32[]{:S(2)}) collective-permute-start(f32[2,1,16,128]{3,2,1,0:T(8,128)S(1)} %get-tuple-element.192), channel_id=1, source_target_pairs={{4,0},{8,4},{12,8},{16,12},{20,16},{24,20},{28,24},{5,1},{9,5},{13... | collective-permute-start | bytes 49160 | tf_op jit(solution)/shard_map/ppermute | solution.py:24
  238.3 6.9 %collective-permute-start.35 = (f32[2,1,16,128]{3,2,1,0:T(8,128)S(1)}, f32[2,1,16,128]{3,2,1,0:T(8,128)S(1)}, u32[]{:S(2)}, u32[]{:S(2)}) collective-permute-start(f32[2,1,16,128]{3,2,1,0:T(8,128)S(1)} %get-tuple-element.191), channel_id=1, source_target_pairs={{0,4},{4,8},{8,12},{12,16},{16,20},{20,24},{24,28},{1,5},{5,9},{9,... | collective-permute-start | bytes 49160 | tf_op jit(solution)/shard_map/ppermute | solution.py:21
  253.0 7.4 %collective-permute-start.38 = (f32[2,1,16,128]{3,2,1,0:T(8,128)S(1)}, f32[2,1,16,128]{3,2,1,0:T(8,128)S(1)}, u32[]{:S(2)}, u32[]{:S(2)}) collective-permute-start(f32[2,1,16,128]{3,2,1,0:T(8,128)S(1)} %get-tuple-element.188), channel_id=1, source_target_pairs={{4,0},{8,4},{12,8},{16,12},{20,16},{24,20},{28,24},{5,1},{9,5},{13... | collective-permute-start | bytes 49160 | tf_op jit(solution)/shard_map/ppermute | solution.py:24
  254.3 6.9 %collective-permute-start.39 = (f32[2,1,16,128]{3,2,1,0:T(8,128)S(1)}, f32[2,1,16,128]{3,2,1,0:T(8,128)S(1)}, u32[]{:S(2)}, u32[]{:S(2)}) collective-permute-start(f32[2,1,16,128]{3,2,1,0:T(8,128)S(1)} %get-tuple-element.187), channel_id=1, source_target_pairs={{0,4},{4,8},{8,12},{12,16},{16,20},{20,24},{24,28},{1,5},{5,9},{9,... | collective-permute-start | bytes 49160 | tf_op jit(solution)/shard_map/ppermute | solution.py:21
  268.9 7.4 %collective-permute-start.42 = (f32[2,1,16,128]{3,2,1,0:T(8,128)S(1)}, f32[2,1,16,128]{3,2,1,0:T(8,128)S(1)}, u32[]{:S(2)}, u32[]{:S(2)}) collective-permute-start(f32[2,1,16,128]{3,2,1,0:T(8,128)S(1)} %get-tuple-element.184), channel_id=1, source_target_pairs={{4,0},{8,4},{12,8},{16,12},{20,16},{24,20},{28,24},{5,1},{9,5},{13... | collective-permute-start | bytes 49160 | tf_op jit(solution)/shard_map/ppermute | solution.py:24
  270.2 6.9 %collective-permute-start.43 = (f32[2,1,16,128]{3,2,1,0:T(8,128)S(1)}, f32[2,1,16,128]{3,2,1,0:T(8,128)S(1)}, u32[]{:S(2)}, u32[]{:S(2)}) collective-permute-start(f32[2,1,16,128]{3,2,1,0:T(8,128)S(1)} %get-tuple-element.183), channel_id=1, source_target_pairs={{0,4},{4,8},{8,12},{12,16},{16,20},{20,24},{24,28},{1,5},{5,9},{9,... | collective-permute-start | bytes 49160 | tf_op jit(solution)/shard_map/ppermute | solution.py:21
  286.0 7.4 %collective-permute-start.46 = (f32[2,1,16,128]{3,2,1,0:T(8,128)S(1)}, f32[2,1,16,128]{3,2,1,0:T(8,128)S(1)}, u32[]{:S(2)}, u32[]{:S(2)}) collective-permute-start(f32[2,1,16,128]{3,2,1,0:T(8,128)S(1)} %get-tuple-element.180), channel_id=1, source_target_pairs={{4,0},{8,4},{12,8},{16,12},{20,16},{24,20},{28,24},{5,1},{9,5},{13... | collective-permute-start | bytes 49160 | tf_op jit(solution)/shard_map/ppermute | solution.py:24
  287.3 6.9 %collective-permute-start.47 = (f32[2,1,16,128]{3,2,1,0:T(8,128)S(1)}, f32[2,1,16,128]{3,2,1,0:T(8,128)S(1)}, u32[]{:S(2)}, u32[]{:S(2)}) collective-permute-start(f32[2,1,16,128]{3,2,1,0:T(8,128)S(1)} %get-tuple-element.179), channel_id=1, source_target_pairs={{0,4},{4,8},{8,12},{12,16},{16,20},{20,24},{24,28},{1,5},{5,9},{9,... | collective-permute-start | bytes 49160 | tf_op jit(solution)/shard_map/ppermute | solution.py:21
  303.0 7.4 %collective-permute-start.50 = (f32[2,1,16,128]{3,2,1,0:T(8,128)S(1)}, f32[2,1,16,128]{3,2,1,0:T(8,128)S(1)}, u32[]{:S(2)}, u32[]{:S(2)}) collective-permute-start(f32[2,1,16,128]{3,2,1,0:T(8,128)S(1)} %get-tuple-element.176), channel_id=1, source_target_pairs={{4,0},{8,4},{12,8},{16,12},{20,16},{24,20},{28,24},{5,1},{9,5},{13... | collective-permute-start | bytes 49160 | tf_op jit(solution)/shard_map/ppermute | solution.py:24
  304.3 6.9 %collective-permute-start.51 = (f32[2,1,16,128]{3,2,1,0:T(8,128)S(1)}, f32[2,1,16,128]{3,2,1,0:T(8,128)S(1)}, u32[]{:S(2)}, u32[]{:S(2)}) collective-permute-start(f32[2,1,16,128]{3,2,1,0:T(8,128)S(1)} %get-tuple-element.175), channel_id=1, source_target_pairs={{0,4},{4,8},{8,12},{12,16},{16,20},{20,24},{24,28},{1,5},{5,9},{9,... | collective-permute-start | bytes 49160 | tf_op jit(solution)/shard_map/ppermute | solution.py:21
  320.1 7.4 %collective-permute-start.54 = (f32[2,1,16,128]{3,2,1,0:T(8,128)S(1)}, f32[2,1,16,128]{3,2,1,0:T(8,128)S(1)}, u32[]{:S(2)}, u32[]{:S(2)}) collective-permute-start(f32[2,1,16,128]{3,2,1,0:T(8,128)S(1)} %get-tuple-element.172), channel_id=1, source_target_pairs={{4,0},{8,4},{12,8},{16,12},{20,16},{24,20},{28,24},{5,1},{9,5},{13... | collective-permute-start | bytes 49160 | tf_op jit(solution)/shard_map/ppermute | solution.py:24
  321.4 6.9 %collective-permute-start.55 = (f32[2,1,16,128]{3,2,1,0:T(8,128)S(1)}, f32[2,1,16,128]{3,2,1,0:T(8,128)S(1)}, u32[]{:S(2)}, u32[]{:S(2)}) collective-permute-start(f32[2,1,16,128]{3,2,1,0:T(8,128)S(1)} %get-tuple-element.171), channel_id=1, source_target_pairs={{0,4},{4,8},{8,12},{12,16},{16,20},{20,24},{24,28},{1,5},{5,9},{9,... | collective-permute-start | bytes 49160 | tf_op jit(solution)/shard_map/ppermute | solution.py:21
  337.2 7.4 %collective-permute-start.58 = (f32[2,1,16,128]{3,2,1,0:T(8,128)S(1)}, f32[2,1,16,128]{3,2,1,0:T(8,128)S(1)}, u32[]{:S(2)}, u32[]{:S(2)}) collective-permute-start(f32[2,1,16,128]{3,2,1,0:T(8,128)S(1)} %get-tuple-element.168), channel_id=1, source_target_pairs={{4,0},{8,4},{12,8},{16,12},{20,16},{24,20},{28,24},{5,1},{9,5},{13... | collective-permute-start | bytes 49160 | tf_op jit(solution)/shard_map/ppermute | solution.py:24
  338.5 6.9 %collective-permute-start.59 = (f32[2,1,16,128]{3,2,1,0:T(8,128)S(1)}, f32[2,1,16,128]{3,2,1,0:T(8,128)S(1)}, u32[]{:S(2)}, u32[]{:S(2)}) collective-permute-start(f32[2,1,16,128]{3,2,1,0:T(8,128)S(1)} %get-tuple-element.167), channel_id=1, source_target_pairs={{0,4},{4,8},{8,12},{12,16},{16,20},{20,24},{24,28},{1,5},{5,9},{9,... | collective-permute-start | bytes 49160 | tf_op jit(solution)/shard_map/ppermute | solution.py:21
  354.3 7.4 %collective-permute-start.62 = (f32[2,1,16,128]{3,2,1,0:T(8,128)S(1)}, f32[2,1,16,128]{3,2,1,0:T(8,128)S(1)}, u32[]{:S(2)}, u32[]{:S(2)}) collective-permute-start(f32[2,1,16,128]{3,2,1,0:T(8,128)S(1)} %get-tuple-element.164), channel_id=1, source_target_pairs={{4,0},{8,4},{12,8},{16,12},{20,16},{24,20},{28,24},{5,1},{9,5},{13... | collective-permute-start | bytes 49160 | tf_op jit(solution)/shard_map/ppermute | solution.py:24
  355.6 6.9 %collective-permute-start.63 = (f32[2,1,16,128]{3,2,1,0:T(8,128)S(1)}, f32[2,1,16,128]{3,2,1,0:T(8,128)S(1)}, u32[]{:S(2)}, u32[]{:S(2)}) collective-permute-start(f32[2,1,16,128]{3,2,1,0:T(8,128)S(1)} %get-tuple-element.163), channel_id=1, source_target_pairs={{0,4},{4,8},{8,12},{12,16},{16,20},{20,24},{24,28},{1,5},{5,9},{9,... | collective-permute-start | bytes 49160 | tf_op jit(solution)/shard_map/ppermute | solution.py:21
  371.4 7.4 %collective-permute-start.66 = (f32[2,1,16,128]{3,2,1,0:T(8,128)S(1)}, f32[2,1,16,128]{3,2,1,0:T(8,128)S(1)}, u32[]{:S(2)}, u32[]{:S(2)}) collective-permute-start(f32[2,1,16,128]{3,2,1,0:T(8,128)S(1)} %get-tuple-element.160), channel_id=1, source_target_pairs={{4,0},{8,4},{12,8},{16,12},{20,16},{24,20},{28,24},{5,1},{9,5},{13... | collective-permute-start | bytes 49160 | tf_op jit(solution)/shard_map/ppermute | solution.py:24
  372.7 6.9 %collective-permute-start.67 = (f32[2,1,16,128]{3,2,1,0:T(8,128)S(1)}, f32[2,1,16,128]{3,2,1,0:T(8,128)S(1)}, u32[]{:S(2)}, u32[]{:S(2)}) collective-permute-start(f32[2,1,16,128]{3,2,1,0:T(8,128)S(1)} %get-tuple-element.159), channel_id=1, source_target_pairs={{0,4},{4,8},{8,12},{12,16},{16,20},{20,24},{24,28},{1,5},{5,9},{9,... | collective-permute-start | bytes 49160 | tf_op jit(solution)/shard_map/ppermute | solution.py:21
  387.4 7.4 %collective-permute-start.70 = (f32[2,1,16,128]{3,2,1,0:T(8,128)S(1)}, f32[2,1,16,128]{3,2,1,0:T(8,128)S(1)}, u32[]{:S(2)}, u32[]{:S(2)}) collective-permute-start(f32[2,1,16,128]{3,2,1,0:T(8,128)S(1)} %get-tuple-element.156), channel_id=1, source_target_pairs={{4,0},{8,4},{12,8},{16,12},{20,16},{24,20},{28,24},{5,1},{9,5},{13... | collective-permute-start | bytes 49160 | tf_op jit(solution)/shard_map/ppermute | solution.py:24
  388.7 6.9 %collective-permute-start.71 = (f32[2,1,16,128]{3,2,1,0:T(8,128)S(1)}, f32[2,1,16,128]{3,2,1,0:T(8,128)S(1)}, u32[]{:S(2)}, u32[]{:S(2)}) collective-permute-start(f32[2,1,16,128]{3,2,1,0:T(8,128)S(1)} %get-tuple-element.155), channel_id=1, source_target_pairs={{0,4},{4,8},{8,12},{12,16},{16,20},{20,24},{24,28},{1,5},{5,9},{9,... | collective-permute-start | bytes 49160 | tf_op jit(solution)/shard_map/ppermute | solution.py:21
  403.3 8.1 %collective-permute-start.74 = (f32[2,1,16,128]{3,2,1,0:T(8,128)S(1)}, f32[2,1,16,128]{3,2,1,0:T(8,128)S(1)}, u32[]{:S(2)}, u32[]{:S(2)}) collective-permute-start(f32[2,1,16,128]{3,2,1,0:T(8,128)S(1)} %get-tuple-element.152), channel_id=1, source_target_pairs={{4,0},{8,4},{12,8},{16,12},{20,16},{24,20},{28,24},{5,1},{9,5},{13... | collective-permute-start | bytes 49160 | tf_op jit(solution)/shard_map/ppermute | solution.py:24
  404.6 6.9 %collective-permute-start.75 = (f32[2,1,16,128]{3,2,1,0:T(8,128)S(1)}, f32[2,1,16,128]{3,2,1,0:T(8,128)S(1)}, u32[]{:S(2)}, u32[]{:S(2)}) collective-permute-start(f32[2,1,16,128]{3,2,1,0:T(8,128)S(1)} %get-tuple-element.151), channel_id=1, source_target_pairs={{0,4},{4,8},{8,12},{12,16},{16,20},{20,24},{24,28},{1,5},{5,9},{9,... | collective-permute-start | bytes 49160 | tf_op jit(solution)/shard_map/ppermute | solution.py:21
  420.4 16.0 %collective-permute-start.78 = (f32[2,1,16,128]{3,2,1,0:T(8,128)}, f32[2,1,16,128]{3,2,1,0:T(8,128)S(1)}, u32[]{:S(2)}, u32[]{:S(2)}) collective-permute-start(f32[2,1,16,128]{3,2,1,0:T(8,128)} %get-tuple-element.148), channel_id=1, source_target_pairs={{4,0},{8,4},{12,8},{16,12},{20,16},{24,20},{28,24},{5,1},{9,5},{13... | collective-permute-start | bytes 49160 | tf_op jit(solution)/shard_map/ppermute | solution.py:24
  421.7 14.7 %collective-permute-start.79 = (f32[2,1,16,128]{3,2,1,0:T(8,128)}, f32[2,1,16,128]{3,2,1,0:T(8,128)}, u32[]{:S(2)}, u32[]{:S(2)}) collective-permute-start(f32[2,1,16,128]{3,2,1,0:T(8,128)} %get-tuple-element.147), channel_id=1, source_target_pairs={{0,4},{4,8},{8,12},{12,16},{16,20},{20,24},{24,28},{1,5},{5,9},{9,... | collective-permute-start | bytes 49160 | tf_op jit(solution)/shard_map/ppermute | solution.py:21
  437.4 7.1 %collective-permute-start.80 = (f32[2,18,1,128]{3,2,1,0:T(1,128)S(1)}, f32[2,18,1,128]{3,2,1,0:T(1,128)S(1)}, u32[]{:S(2)}, u32[]{:S(2)}) collective-permute-start(f32[2,18,1,128]{3,2,1,0:T(1,128)S(1)} %get-tuple-element.89), channel_id=1, source_target_pairs={{1,0},{2,1},{3,2},{5,4},{6,5},{7,6},{9,8},{10,9},{11,10},{13,12},{... | collective-permute-start | bytes 55304 | tf_op jit(solution)/shard_map/ppermute | solution.py:24
  448.9 25.9 %collective-permute-start.82 = (f32[2,1,16,128]{3,2,1,0:T(8,128)}, f32[2,1,16,128]{3,2,1,0:T(8,128)S(1)}, u32[]{:S(2)}, u32[]{:S(2)}) collective-permute-start(f32[2,1,16,128]{3,2,1,0:T(8,128)} %get-tuple-element.144), channel_id=1, source_target_pairs={{4,0},{8,4},{12,8},{16,12},{20,16},{24,20},{28,24},{5,1},{9,5},{13... | collective-permute-start | bytes 49160 | tf_op jit(solution)/shard_map/ppermute | solution.py:24
  450.2 24.6 %collective-permute-start.83 = (f32[2,1,16,128]{3,2,1,0:T(8,128)}, f32[2,1,16,128]{3,2,1,0:T(8,128)}, u32[]{:S(2)}, u32[]{:S(2)}) collective-permute-start(f32[2,1,16,128]{3,2,1,0:T(8,128)} %get-tuple-element.143), channel_id=1, source_target_pairs={{0,4},{4,8},{8,12},{12,16},{16,20},{20,24},{24,28},{1,5},{5,9},{9,... | collective-permute-start | bytes 49160 | tf_op jit(solution)/shard_map/ppermute | solution.py:21
  475.7 7.1 %collective-permute-start.84 = (f32[2,18,1,128]{3,2,1,0:T(1,128)S(1)}, f32[2,18,1,128]{3,2,1,0:T(1,128)S(1)}, u32[]{:S(2)}, u32[]{:S(2)}) collective-permute-start(f32[2,18,1,128]{3,2,1,0:T(1,128)S(1)} %get-tuple-element.87), channel_id=1, source_target_pairs={{1,0},{2,1},{3,2},{5,4},{6,5},{7,6},{9,8},{10,9},{11,10},{13,12},{... | collective-permute-start | bytes 55304 | tf_op jit(solution)/shard_map/ppermute | solution.py:24
  486.0 8.4 %collective-permute-start.86 = (f32[2,1,16,128]{3,2,1,0:T(8,128)S(1)}, f32[2,1,16,128]{3,2,1,0:T(8,128)S(1)}, u32[]{:S(2)}, u32[]{:S(2)}) collective-permute-start(f32[2,1,16,128]{3,2,1,0:T(8,128)S(1)} %get-tuple-element.140), channel_id=1, source_target_pairs={{4,0},{8,4},{12,8},{16,12},{20,16},{24,20},{28,24},{5,1},{9,5},{13... | collective-permute-start | bytes 49160 | tf_op jit(solution)/shard_map/ppermute | solution.py:24
  487.3 7.2 %collective-permute-start.87 = (f32[2,1,16,128]{3,2,1,0:T(8,128)S(1)}, f32[2,1,16,128]{3,2,1,0:T(8,128)S(1)}, u32[]{:S(2)}, u32[]{:S(2)}) collective-permute-start(f32[2,1,16,128]{3,2,1,0:T(8,128)S(1)} %get-tuple-element.139), channel_id=1, source_target_pairs={{0,4},{4,8},{8,12},{12,16},{16,20},{20,24},{24,28},{1,5},{5,9},{9,... | collective-permute-start | bytes 49160 | tf_op jit(solution)/shard_map/ppermute | solution.py:21
  495.8 6.0 collective-permute-start.89
  504.4 25.8 %collective-permute-start.90 = (f32[2,1,16,128]{3,2,1,0:T(8,128)}, f32[2,1,16,128]{3,2,1,0:T(8,128)S(1)}, u32[]{:S(2)}, u32[]{:S(2)}) collective-permute-start(f32[2,1,16,128]{3,2,1,0:T(8,128)} %get-tuple-element.136), channel_id=1, source_target_pairs={{4,0},{8,4},{12,8},{16,12},{20,16},{24,20},{28,24},{5,1},{9,5},{13... | collective-permute-start | bytes 49160 | tf_op jit(solution)/shard_map/ppermute | solution.py:24
  505.7 24.6 %collective-permute-start.91 = (f32[2,1,16,128]{3,2,1,0:T(8,128)}, f32[2,1,16,128]{3,2,1,0:T(8,128)}, u32[]{:S(2)}, u32[]{:S(2)}) collective-permute-start(f32[2,1,16,128]{3,2,1,0:T(8,128)} %get-tuple-element.135), channel_id=1, source_target_pairs={{0,4},{4,8},{8,12},{12,16},{16,20},{20,24},{24,28},{1,5},{5,9},{9,... | collective-permute-start | bytes 49160 | tf_op jit(solution)/shard_map/ppermute | solution.py:21
  531.2 7.1 %collective-permute-start.92 = (f32[2,18,1,128]{3,2,1,0:T(1,128)S(1)}, f32[2,18,1,128]{3,2,1,0:T(1,128)S(1)}, u32[]{:S(2)}, u32[]{:S(2)}) collective-permute-start(f32[2,18,1,128]{3,2,1,0:T(1,128)S(1)} %get-tuple-element.83), channel_id=1, source_target_pairs={{1,0},{2,1},{3,2},{5,4},{6,5},{7,6},{9,8},{10,9},{11,10},{13,12},{... | collective-permute-start | bytes 55304 | tf_op jit(solution)/shard_map/ppermute | solution.py:24
  541.5 6.9 %collective-permute-start.94 = (f32[2,1,16,128]{3,2,1,0:T(8,128)S(1)}, f32[2,1,16,128]{3,2,1,0:T(8,128)S(1)}, u32[]{:S(2)}, u32[]{:S(2)}) collective-permute-start(f32[2,1,16,128]{3,2,1,0:T(8,128)S(1)} %get-tuple-element.132), channel_id=1, source_target_pairs={{4,0},{8,4},{12,8},{16,12},{20,16},{24,20},{28,24},{5,1},{9,5},{13... | collective-permute-start | bytes 49160 | tf_op jit(solution)/shard_map/ppermute | solution.py:24
  (87 other events, 1642.8 us)
where the time goes:
time: 625 us; the launch traced here: 621 us
  starting transfers between devices  304 us (49%)
  blocking collectives  119 us (19%)
  local copies, waits for them, and re-layouts  93.1 us (15%)
  other arithmetic  58.7 us (9%)
  waiting for transfers between devices  41.7 us (7%)
    ppermute x48, starting transfers between devices, padded_2(): lax.ppermute(lax.slice_in_dim(block, block.shape[dim] - width, None, axis...  240 us
    all_gather x1, blocking collectives, local(): all_rows = lax.all_gather(effective, ('gx', 'gy'), axis=0, tiled=True)  71.9 us
    ppermute x48, starting transfers between devices, padded_2(): lax.ppermute(lax.slice_in_dim(block, 0, width, axis=dim), axis, backward)  62 us
    unnamed x1, blocking collectives  47.6 us
    ppermute x48, waiting for transfers between devices, padded_2(): lax.ppermute(lax.slice_in_dim(block, block.shape[dim] - width, None, axis...  41.6 us
    slice x1, local copies, waits for them, and re-layouts, local(): right_a = grad_p[step_index] + sources[step_index] + acc_p * multipliers[0]  30.5 us
    another operation x3, local copies, waits for them, and re-layouts, relax(): return jnp.stack([new_a, new_b])  26.2 us
    add x23, other arithmetic, relax(): new_b = old_b + table[16] * (table[7] - out_b)  22.6 us
  transfers between devices with their start and end apart: 98, of which 42 were waited for; matrix products, arithmetic and copies ran while one was open for 15% of the time, Pallas kernels for 0%

commit v1 on v0

--- a/solution.py
+++ b/solution.py
@@ -93,7 +93,26 @@
     w_down = jnp.where(first_z, trans_z, 0.0)
     weight_sum = w_east + w_west + w_north + w_south + w_up + w_down
     effective = jnp.where(control == 1, rate_mis, bhp_mis)
-    all_rows = lax.all_gather(effective, ("gx", "gy"), axis=0, tiled=True)
+    s_next, y_new, part_next = (
+        lax.axis_size(("gx", "gy")),
+        lax.axis_index(("gx", "gy")),
+        effective.shape[0],
+    )
+    block_out, r2 = (effective, 1)
+    while r2 < s_next:
+        block_out = jnp.concatenate(
+            [
+                block_out,
+                lax.ppermute(
+                    block_out,
+                    axis_name=("gx", "gy"),
+                    perm=[(src_i, (src_i - r2) % s_next) for src_i in range(s_next)],
+                ),
+            ],
+            axis=0,
+        )
+        r2 = 2 * r2
+    all_rows = jnp.roll(block_out, y_new * part_next, axis=0)
     well_count = all_rows.shape[0]
     selector = (perf_well[:, None] == jnp.arange(well_count, dtype=jnp.int32)[None, :]).astype(
         jnp.float32

time: 625 us -> 583 us (0.933)
  blocking collectives: 119 us -> 45.2 us
  starting transfers between devices: 304 us -> 317 us
  waiting for transfers between devices: 41.7 us -> 52.4 us
    all_gather x1 -> x0, blocking collectives: 71.9 us -> none  [local(): all_rows = lax.all_gather(effective, ('gx', 'gy'), axis=0, tiled=True)]
    ppermute x0 -> x5, starting transfers between devices: none -> 13.3 us  [local(): lax.ppermute(block_out, axis_name=('gx', 'gy'), perm=[(src_i, (src_i - r2...]
  transfers between devices with their start and end apart: 98 -> 103, of which waited for: 42 -> 48; matrix products, arithmetic and copies ran while one was open for 15% -> 18% of each run, Pallas kernels for 0% -> 0%
where the time goes in v1:
time: 583 us; the launch traced here: 579 us
  starting transfers between devices  317 us (54%)
  local copies, waits for them, and re-layouts  98.3 us (17%)
  other arithmetic  61.7 us (11%)
  waiting for transfers between devices  52.4 us (9%)
  blocking collectives  45.2 us (8%)
    ppermute x48, starting transfers between devices, padded_2(): lax.ppermute(lax.slice_in_dim(block, block.shape[dim] - width, None, axis...  239 us
    ppermute x48, starting transfers between devices, padded_2(): lax.ppermute(lax.slice_in_dim(block, 0, width, axis=dim), axis, backward)  62.2 us
    unnamed x1, blocking collectives  45.2 us
    ppermute x48, waiting for transfers between devices, padded_2(): lax.ppermute(lax.slice_in_dim(block, block.shape[dim] - width, None, axis...  40.3 us
    slice x1, local copies, waits for them, and re-layouts, local(): right_a = grad_p[step_index] + sources[step_index] + acc_p * multipliers[0]  30.4 us
    another operation x3, local copies, waits for them, and re-layouts, relax(): return jnp.stack([new_a, new_b])  26 us
    add x23, other arithmetic, relax(): new_b = old_b + table[16] * (table[7] - out_b)  22.7 us
    gather x3, local copies, waits for them, and re-layouts, local(): at_cells = flat_fields[:, perf_cell]  20.8 us
  transfers between devices with their start and end apart: 103, of which 48 were waited for; matrix products, arithmetic and copies ran while one was open for 18% of the time, Pallas kernels for 0%

profile of v1, /device:TPU:0, one launch (start us, length us, event | category | flops | bytes accessed | tf_op | source)
XLA Modules:
  0.0 578.8 jit_solution(2827435444961159838)
XLA Ops:
  8.5 5.3 collective-permute-start.2
  36.9 7.8 %scatter_custom_fusion = f32[3,32768]{0,1:T(8,128)} fusion(s32[128]{0:T(128)S(1)} %compare_select_fusion, f32[128,3]{1,0:T(8,128)S(1)} %copy.33, f32[]{:T(128)} %constant.22.clone.1), kind=kCustom, calls=%fused_computation.10 | custom fusion | flops 384 | bytes 393220 | tf_op jit(solution)/shard_map/scatter-add | solution.py:124
  44.9 30.4 %slice_reduce_fusion = (f32[32768]{0:T(1024)S(1)}, f32[32768]{0:T(1024)S(1)}, f32[32768]{0:T(1024)S(1)}) fusion(f32[3,32768]{0,1:T(8,128)} %scatter_custom_fusion), kind=kLoop, calls=%fused_computation.7 | loop fusion | bytes 786432 | tf_op jit(solution)/shard_map/slice | solution.py:130
  95.5 4.5 collective-permute-start.14
  108.4 5.0 collective-permute-start.18
  117.7 4.6 collective-permute-start.20
  124.4 4.7 collective-permute-start.22
  133.3 5.1 collective-permute-start.24
  140.6 4.5 collective-permute-start.26
  149.5 5.1 collective-permute-start.28
  156.8 4.5 collective-permute-start.30
  165.7 5.1 collective-permute-start.32
  173.0 4.5 collective-permute-start.34
  181.8 5.1 collective-permute-start.36
  189.1 4.5 collective-permute-start.38
  198.0 5.1 collective-permute-start.40
  205.3 4.5 collective-permute-start.42
  213.1 5.9 %collective-permute-start.44 = (f32[2,1,16,128]{3,2,1,0:T(8,128)S(1)}, f32[2,1,16,128]{3,2,1,0:T(8,128)S(1)}, u32[]{:S(2)}, u32[]{:S(2)}) collective-permute-start(f32[2,1,16,128]{3,2,1,0:T(8,128)S(1)} %get-tuple-element.187), channel_id=1, source_target_pairs={{0,4},{4,8},{8,12},{12,16},{16,20},{20,24},{24,28},{1,5},{5,9},{9,... | collective-permute-start | bytes 49160 | tf_op jit(solution)/shard_map/ppermute | solution.py:21
  221.2 4.5 collective-permute-start.46
  228.8 6.0 %collective-permute-start.48 = (f32[2,1,16,128]{3,2,1,0:T(8,128)S(1)}, f32[2,1,16,128]{3,2,1,0:T(8,128)S(1)}, u32[]{:S(2)}, u32[]{:S(2)}) collective-permute-start(f32[2,1,16,128]{3,2,1,0:T(8,128)S(1)} %get-tuple-element.183), channel_id=1, source_target_pairs={{0,4},{4,8},{8,12},{12,16},{16,20},{20,24},{24,28},{1,5},{5,9},{9,... | collective-permute-start | bytes 49160 | tf_op jit(solution)/shard_map/ppermute | solution.py:21
  237.0 4.5 collective-permute-start.50
  245.9 6.0 %collective-permute-start.52 = (f32[2,1,16,128]{3,2,1,0:T(8,128)S(1)}, f32[2,1,16,128]{3,2,1,0:T(8,128)S(1)}, u32[]{:S(2)}, u32[]{:S(2)}) collective-permute-start(f32[2,1,16,128]{3,2,1,0:T(8,128)S(1)} %get-tuple-element.179), channel_id=1, source_target_pairs={{0,4},{4,8},{8,12},{12,16},{16,20},{20,24},{24,28},{1,5},{5,9},{9,... | collective-permute-start | bytes 49160 | tf_op jit(solution)/shard_map/ppermute | solution.py:21
  254.1 4.5 collective-permute-start.54
  263.0 6.0 %collective-permute-start.56 = (f32[2,1,16,128]{3,2,1,0:T(8,128)S(1)}, f32[2,1,16,128]{3,2,1,0:T(8,128)S(1)}, u32[]{:S(2)}, u32[]{:S(2)}) collective-permute-start(f32[2,1,16,128]{3,2,1,0:T(8,128)S(1)} %get-tuple-element.175), channel_id=1, source_target_pairs={{0,4},{4,8},{8,12},{12,16},{16,20},{20,24},{24,28},{1,5},{5,9},{9,... | collective-permute-start | bytes 49160 | tf_op jit(solution)/shard_map/ppermute | solution.py:21
  271.2 4.5 collective-permute-start.58
  280.1 6.0 %collective-permute-start.60 = (f32[2,1,16,128]{3,2,1,0:T(8,128)S(1)}, f32[2,1,16,128]{3,2,1,0:T(8,128)S(1)}, u32[]{:S(2)}, u32[]{:S(2)}) collective-permute-start(f32[2,1,16,128]{3,2,1,0:T(8,128)S(1)} %get-tuple-element.171), channel_id=1, source_target_pairs={{0,4},{4,8},{8,12},{12,16},{16,20},{20,24},{24,28},{1,5},{5,9},{9,... | collective-permute-start | bytes 49160 | tf_op jit(solution)/shard_map/ppermute | solution.py:21
  288.3 4.5 collective-permute-start.62
  297.2 6.0 %collective-permute-start.64 = (f32[2,1,16,128]{3,2,1,0:T(8,128)S(1)}, f32[2,1,16,128]{3,2,1,0:T(8,128)S(1)}, u32[]{:S(2)}, u32[]{:S(2)}) collective-permute-start(f32[2,1,16,128]{3,2,1,0:T(8,128)S(1)} %get-tuple-element.167), channel_id=1, source_target_pairs={{0,4},{4,8},{8,12},{12,16},{16,20},{20,24},{24,28},{1,5},{5,9},{9,... | collective-permute-start | bytes 49160 | tf_op jit(solution)/shard_map/ppermute | solution.py:21
  314.3 6.0 %collective-permute-start.68 = (f32[2,1,16,128]{3,2,1,0:T(8,128)S(1)}, f32[2,1,16,128]{3,2,1,0:T(8,128)S(1)}, u32[]{:S(2)}, u32[]{:S(2)}) collective-permute-start(f32[2,1,16,128]{3,2,1,0:T(8,128)S(1)} %get-tuple-element.163), channel_id=1, source_target_pairs={{0,4},{4,8},{8,12},{12,16},{16,20},{20,24},{24,28},{1,5},{5,9},{9,... | collective-permute-start | bytes 49160 | tf_op jit(solution)/shard_map/ppermute | solution.py:21
  331.4 6.0 %collective-permute-start.72 = (f32[2,1,16,128]{3,2,1,0:T(8,128)S(1)}, f32[2,1,16,128]{3,2,1,0:T(8,128)S(1)}, u32[]{:S(2)}, u32[]{:S(2)}) collective-permute-start(f32[2,1,16,128]{3,2,1,0:T(8,128)S(1)} %get-tuple-element.159), channel_id=1, source_target_pairs={{0,4},{4,8},{8,12},{12,16},{16,20},{20,24},{24,28},{1,5},{5,9},{9,... | collective-permute-start | bytes 49160 | tf_op jit(solution)/shard_map/ppermute | solution.py:21
  339.6 4.5 collective-permute-start.74
  347.4 6.0 %collective-permute-start.76 = (f32[2,1,16,128]{3,2,1,0:T(8,128)S(1)}, f32[2,1,16,128]{3,2,1,0:T(8,128)S(1)}, u32[]{:S(2)}, u32[]{:S(2)}) collective-permute-start(f32[2,1,16,128]{3,2,1,0:T(8,128)S(1)} %get-tuple-element.155), channel_id=1, source_target_pairs={{0,4},{4,8},{8,12},{12,16},{16,20},{20,24},{24,28},{1,5},{5,9},{9,... | collective-permute-start | bytes 49160 | tf_op jit(solution)/shard_map/ppermute | solution.py:21
  363.3 6.0 %collective-permute-start.80 = (f32[2,1,16,128]{3,2,1,0:T(8,128)S(1)}, f32[2,1,16,128]{3,2,1,0:T(8,128)S(1)}, u32[]{:S(2)}, u32[]{:S(2)}) collective-permute-start(f32[2,1,16,128]{3,2,1,0:T(8,128)S(1)} %get-tuple-element.151), channel_id=1, source_target_pairs={{0,4},{4,8},{8,12},{12,16},{16,20},{20,24},{24,28},{1,5},{5,9},{9,... | collective-permute-start | bytes 49160 | tf_op jit(solution)/shard_map/ppermute | solution.py:21
  380.6 6.6 %collective-permute-start.84 = (f32[2,1,16,128]{3,2,1,0:T(8,128)}, f32[2,1,16,128]{3,2,1,0:T(8,128)}, u32[]{:S(2)}, u32[]{:S(2)}) collective-permute-start(f32[2,1,16,128]{3,2,1,0:T(8,128)} %get-tuple-element.147), channel_id=1, source_target_pairs={{0,4},{4,8},{8,12},{12,16},{16,20},{20,24},{24,28},{1,5},{5,9},{9,... | collective-permute-start | bytes 49160 | tf_op jit(solution)/shard_map/ppermute | solution.py:21
  397.6 4.5 collective-permute-start.86
  409.2 6.4 %collective-permute-start.88 = (f32[2,1,16,128]{3,2,1,0:T(8,128)}, f32[2,1,16,128]{3,2,1,0:T(8,128)}, u32[]{:S(2)}, u32[]{:S(2)}) collective-permute-start(f32[2,1,16,128]{3,2,1,0:T(8,128)} %get-tuple-element.143), channel_id=1, source_target_pairs={{0,4},{4,8},{8,12},{12,16},{16,20},{20,24},{24,28},{1,5},{5,9},{9,... | collective-permute-start | bytes 49160 | tf_op jit(solution)/shard_map/ppermute | solution.py:21
  417.5 8.8 %copy.36 = f32[2,32768]{0,1:T(8,128)} copy(f32[2,32768]{1,0:T(2,128)} %pad_maximum_fusion.307) | data formatting | bytes 524288 | tf_op jit(solution)/shard_map/stack | solution.py:53
  426.4 7.1 %gather_fusion.4 = f32[128,2]{1,0:T(8,128)} fusion(f32[2,32768]{0,1:T(8,128)} %copy.36, s32[1024]{0:T(1024)} %pad_clamp_fusion), kind=kCustom, calls=%fused_computation.4 | custom fusion | bytes 2560 | tf_op jit(solution)/shard_map/gather | solution.py:159
  435.8 4.5 collective-permute-start.90
  446.0 5.5 collective-permute-start.92
  454.5 4.6 collective-permute-start.94
  464.3 6.6 %collective-permute-start.96 = (f32[2,1,16,128]{3,2,1,0:T(8,128)}, f32[2,1,16,128]{3,2,1,0:T(8,128)}, u32[]{:S(2)}, u32[]{:S(2)}) collective-permute-start(f32[2,1,16,128]{3,2,1,0:T(8,128)} %get-tuple-element.135), channel_id=1, source_target_pairs={{0,4},{4,8},{8,12},{12,16},{16,20},{20,24},{24,28},{1,5},{5,9},{9,... | collective-permute-start | bytes 49160 | tf_op jit(solution)/shard_map/ppermute | solution.py:21
  472.9 8.8 %copy.35 = f32[2,32768]{0,1:T(8,128)} copy(f32[2,32768]{1,0:T(2,128)} %pad_maximum_fusion.306) | data formatting | bytes 524288 | tf_op jit(solution)/shard_map/stack | solution.py:53
  481.7 7.1 %gather_fusion.2 = f32[128,2]{1,0:T(8,128)} fusion(f32[2,32768]{0,1:T(8,128)} %copy.35, s32[1024]{0:T(1024)} %pad_clamp_fusion), kind=kCustom, calls=%fused_computation.2 | custom fusion | bytes 2560 | tf_op jit(solution)/shard_map/gather | solution.py:159
  509.6 4.8 collective-permute-start.102
  517.6 8.3 %copy.34 = f32[2,32768]{0,1:T(8,128)} copy(f32[2,32768]{1,0:T(2,128)S(1)} %pad_maximum_fusion.305) | data formatting | bytes 524288 | tf_op jit(solution)/shard_map/stack | solution.py:53
  525.9 6.5 %gather_fusion = f32[128,2]{1,0:T(8,128)S(1)} fusion(f32[2,32768]{0,1:T(8,128)} %copy.34, s32[1024]{0:T(1024)} %pad_clamp_fusion), kind=kCustom, calls=%fused_computation | custom fusion | bytes 2560 | tf_op jit(solution)/shard_map/gather | solution.py:159
  533.0 45.2 %all-reduce.51 = f32[64,3]{1,0:T(8,128)S(1)} all-reduce(f32[64,3]{1,0:T(8,128)S(1)} %fusion.588), channel_id=2, replica_groups=mesh['gx'=8,'gy'=4] {'gx','gy'}, use_global_device_ids=true, to_apply=%region_1.2.clone | all-reduce | flops 192 | bytes 1536
  (413 shorter events, 241.9 us)
Async XLA Ops:
  1.2 75.7 %collective-permute-start.7 = (f32[2,1,16,128]{3,2,1,0:T(8,128)}, f32[2,1,16,128]{3,2,1,0:T(8,128)S(1)}, u32[]{:S(2)}, u32[]{:S(2)}) collective-permute-start(f32[2,1,16,128]{3,2,1,0:T(8,128)} %broadcast.164), channel_id=1, source_target_pairs={{4,0},{8,4},{12,8},{16,12},{20,16},{24,20},{28,24},{5,1},{9,5},{13... | collective-permute-start | bytes 49160 | tf_op jit(solution)/shard_map/ppermute | solution.py:24
  2.5 74.4 %collective-permute-start.8 = (f32[2,1,16,128]{3,2,1,0:T(8,128)}, f32[2,1,16,128]{3,2,1,0:T(8,128)}, u32[]{:S(2)}, u32[]{:S(2)}) collective-permute-start(f32[2,1,16,128]{3,2,1,0:T(8,128)} %broadcast.164), channel_id=1, source_target_pairs={{0,4},{4,8},{8,12},{12,16},{16,20},{20,24},{24,28},{1,5},{5,9},{9,... | collective-permute-start | bytes 49160 | tf_op jit(solution)/shard_map/ppermute | solution.py:21
  8.5 12.2 %collective-permute-start.2 = (f32[2,3]{0,1:T(4,128)S(1)}, f32[2,3]{0,1:T(4,128)S(1)}, u32[]{:S(2)}, u32[]{:S(2)}) collective-permute-start(f32[2,3]{0,1:T(4,128)S(1)} %compare_select_fusion.1), channel_id=1, source_target_pairs={{0,31},{1,0},{2,1},{3,2},{4,3},{5,4},{6,5},{7,6},{8,7},{9,8},{10,9... | collective-permute-start | bytes 80 | tf_op jit(solution)/shard_map/ppermute | solution.py:106
  14.5 60.9 %collective-permute-start = (f32[1,16,128]{2,1,0:T(8,128)S(1)}, f32[1,16,128]{2,1,0:T(8,128)S(1)}, u32[]{:S(2)}, u32[]{:S(2)}) collective-permute-start(f32[1,16,128]{2,1,0:T(8,128)S(1)} %slice.1103), channel_id=1, source_target_pairs={{4,0},{8,4},{12,8},{16,12},{20,16},{24,20},{28,24},{5,1},{9,5},{13... | collective-permute-start | bytes 24584 | tf_op jit(solution)/shard_map/ppermute | solution.py:13
  16.6 58.8 %collective-permute-start.1 = (f32[16,1,128]{2,1,0:T(1,128)S(1)}, f32[16,1,128]{2,1,0:T(1,128)S(1)}, u32[]{:S(2)}, u32[]{:S(2)}) collective-permute-start(f32[16,1,128]{2,1,0:T(1,128)S(1)} %slice.1105), channel_id=1, source_target_pairs={{1,0},{2,1},{3,2},{5,4},{6,5},{7,6},{9,8},{10,9},{11,10},{13,12},{... | collective-permute-start | bytes 24584 | tf_op jit(solution)/shard_map/ppermute | solution.py:13
  95.5 6.0 %collective-permute-start.14 = (f32[2,18,1,128]{3,2,1,0:T(1,128)S(1)}, f32[2,18,1,128]{3,2,1,0:T(1,128)S(1)}, u32[]{:S(2)}, u32[]{:S(2)}) collective-permute-start(f32[2,18,1,128]{3,2,1,0:T(1,128)S(1)} %get-tuple-element.126), channel_id=1, source_target_pairs={{0,1},{1,2},{2,3},{4,5},{5,6},{6,7},{8,9},{9,10},{10,11},{12,13},{... | collective-permute-start | bytes 55304 | tf_op jit(solution)/shard_map/ppermute | solution.py:21
  107.1 6.5 %collective-permute-start.17 = (f32[2,18,1,128]{3,2,1,0:T(1,128)S(1)}, f32[2,18,1,128]{3,2,1,0:T(1,128)S(1)}, u32[]{:S(2)}, u32[]{:S(2)}) collective-permute-start(f32[2,18,1,128]{3,2,1,0:T(1,128)S(1)} %get-tuple-element.123), channel_id=1, source_target_pairs={{1,0},{2,1},{3,2},{5,4},{6,5},{7,6},{9,8},{10,9},{11,10},{13,12},{... | collective-permute-start | bytes 55304 | tf_op jit(solution)/shard_map/ppermute | solution.py:24
  108.4 6.5 %collective-permute-start.18 = (f32[2,18,1,128]{3,2,1,0:T(1,128)S(1)}, f32[2,18,1,128]{3,2,1,0:T(1,128)S(1)}, u32[]{:S(2)}, u32[]{:S(2)}) collective-permute-start(f32[2,18,1,128]{3,2,1,0:T(1,128)S(1)} %get-tuple-element.124), channel_id=1, source_target_pairs={{0,1},{1,2},{2,3},{4,5},{5,6},{6,7},{8,9},{9,10},{10,11},{12,13},{... | collective-permute-start | bytes 55304 | tf_op jit(solution)/shard_map/ppermute | solution.py:21
  123.1 6.2 %collective-permute-start.21 = (f32[2,18,1,128]{3,2,1,0:T(1,128)S(1)}, f32[2,18,1,128]{3,2,1,0:T(1,128)S(1)}, u32[]{:S(2)}, u32[]{:S(2)}) collective-permute-start(f32[2,18,1,128]{3,2,1,0:T(1,128)S(1)} %get-tuple-element.121), channel_id=1, source_target_pairs={{1,0},{2,1},{3,2},{5,4},{6,5},{7,6},{9,8},{10,9},{11,10},{13,12},{... | collective-permute-start | bytes 55304 | tf_op jit(solution)/shard_map/ppermute | solution.py:24
  132.0 6.5 %collective-permute-start.23 = (f32[2,1,16,128]{3,2,1,0:T(8,128)S(1)}, f32[2,1,16,128]{3,2,1,0:T(8,128)S(1)}, u32[]{:S(2)}, u32[]{:S(2)}) collective-permute-start(f32[2,1,16,128]{3,2,1,0:T(8,128)S(1)} %get-tuple-element.208), channel_id=1, source_target_pairs={{4,0},{8,4},{12,8},{16,12},{20,16},{24,20},{28,24},{5,1},{9,5},{13... | collective-permute-start | bytes 49160 | tf_op jit(solution)/shard_map/ppermute | solution.py:24
  148.2 6.5 %collective-permute-start.27 = (f32[2,1,16,128]{3,2,1,0:T(8,128)S(1)}, f32[2,1,16,128]{3,2,1,0:T(8,128)S(1)}, u32[]{:S(2)}, u32[]{:S(2)}) collective-permute-start(f32[2,1,16,128]{3,2,1,0:T(8,128)S(1)} %get-tuple-element.204), channel_id=1, source_target_pairs={{4,0},{8,4},{12,8},{16,12},{20,16},{24,20},{28,24},{5,1},{9,5},{13... | collective-permute-start | bytes 49160 | tf_op jit(solution)/shard_map/ppermute | solution.py:24
  164.4 6.5 %collective-permute-start.31 = (f32[2,1,16,128]{3,2,1,0:T(8,128)S(1)}, f32[2,1,16,128]{3,2,1,0:T(8,128)S(1)}, u32[]{:S(2)}, u32[]{:S(2)}) collective-permute-start(f32[2,1,16,128]{3,2,1,0:T(8,128)S(1)} %get-tuple-element.200), channel_id=1, source_target_pairs={{4,0},{8,4},{12,8},{16,12},{20,16},{24,20},{28,24},{5,1},{9,5},{13... | collective-permute-start | bytes 49160 | tf_op jit(solution)/shard_map/ppermute | solution.py:24
  180.5 6.5 %collective-permute-start.35 = (f32[2,1,16,128]{3,2,1,0:T(8,128)S(1)}, f32[2,1,16,128]{3,2,1,0:T(8,128)S(1)}, u32[]{:S(2)}, u32[]{:S(2)}) collective-permute-start(f32[2,1,16,128]{3,2,1,0:T(8,128)S(1)} %get-tuple-element.196), channel_id=1, source_target_pairs={{4,0},{8,4},{12,8},{16,12},{20,16},{24,20},{28,24},{5,1},{9,5},{13... | collective-permute-start | bytes 49160 | tf_op jit(solution)/shard_map/ppermute | solution.py:24
  196.7 6.5 %collective-permute-start.39 = (f32[2,1,16,128]{3,2,1,0:T(8,128)S(1)}, f32[2,1,16,128]{3,2,1,0:T(8,128)S(1)}, u32[]{:S(2)}, u32[]{:S(2)}) collective-permute-start(f32[2,1,16,128]{3,2,1,0:T(8,128)S(1)} %get-tuple-element.192), channel_id=1, source_target_pairs={{4,0},{8,4},{12,8},{16,12},{20,16},{24,20},{28,24},{5,1},{9,5},{13... | collective-permute-start | bytes 49160 | tf_op jit(solution)/shard_map/ppermute | solution.py:24
  211.8 7.2 %collective-permute-start.43 = (f32[2,1,16,128]{3,2,1,0:T(8,128)S(1)}, f32[2,1,16,128]{3,2,1,0:T(8,128)S(1)}, u32[]{:S(2)}, u32[]{:S(2)}) collective-permute-start(f32[2,1,16,128]{3,2,1,0:T(8,128)S(1)} %get-tuple-element.188), channel_id=1, source_target_pairs={{4,0},{8,4},{12,8},{16,12},{20,16},{24,20},{28,24},{5,1},{9,5},{13... | collective-permute-start | bytes 49160 | tf_op jit(solution)/shard_map/ppermute | solution.py:24
  213.1 6.7 %collective-permute-start.44 = (f32[2,1,16,128]{3,2,1,0:T(8,128)S(1)}, f32[2,1,16,128]{3,2,1,0:T(8,128)S(1)}, u32[]{:S(2)}, u32[]{:S(2)}) collective-permute-start(f32[2,1,16,128]{3,2,1,0:T(8,128)S(1)} %get-tuple-element.187), channel_id=1, source_target_pairs={{0,4},{4,8},{8,12},{12,16},{16,20},{20,24},{24,28},{1,5},{5,9},{9,... | collective-permute-start | bytes 49160 | tf_op jit(solution)/shard_map/ppermute | solution.py:21
  227.5 7.4 %collective-permute-start.47 = (f32[2,1,16,128]{3,2,1,0:T(8,128)S(1)}, f32[2,1,16,128]{3,2,1,0:T(8,128)S(1)}, u32[]{:S(2)}, u32[]{:S(2)}) collective-permute-start(f32[2,1,16,128]{3,2,1,0:T(8,128)S(1)} %get-tuple-element.184), channel_id=1, source_target_pairs={{4,0},{8,4},{12,8},{16,12},{20,16},{24,20},{28,24},{5,1},{9,5},{13... | collective-permute-start | bytes 49160 | tf_op jit(solution)/shard_map/ppermute | solution.py:24
  228.8 6.9 %collective-permute-start.48 = (f32[2,1,16,128]{3,2,1,0:T(8,128)S(1)}, f32[2,1,16,128]{3,2,1,0:T(8,128)S(1)}, u32[]{:S(2)}, u32[]{:S(2)}) collective-permute-start(f32[2,1,16,128]{3,2,1,0:T(8,128)S(1)} %get-tuple-element.183), channel_id=1, source_target_pairs={{0,4},{4,8},{8,12},{12,16},{16,20},{20,24},{24,28},{1,5},{5,9},{9,... | collective-permute-start | bytes 49160 | tf_op jit(solution)/shard_map/ppermute | solution.py:21
  244.6 7.4 %collective-permute-start.51 = (f32[2,1,16,128]{3,2,1,0:T(8,128)S(1)}, f32[2,1,16,128]{3,2,1,0:T(8,128)S(1)}, u32[]{:S(2)}, u32[]{:S(2)}) collective-permute-start(f32[2,1,16,128]{3,2,1,0:T(8,128)S(1)} %get-tuple-element.180), channel_id=1, source_target_pairs={{4,0},{8,4},{12,8},{16,12},{20,16},{24,20},{28,24},{5,1},{9,5},{13... | collective-permute-start | bytes 49160 | tf_op jit(solution)/shard_map/ppermute | solution.py:24
  245.9 6.9 %collective-permute-start.52 = (f32[2,1,16,128]{3,2,1,0:T(8,128)S(1)}, f32[2,1,16,128]{3,2,1,0:T(8,128)S(1)}, u32[]{:S(2)}, u32[]{:S(2)}) collective-permute-start(f32[2,1,16,128]{3,2,1,0:T(8,128)S(1)} %get-tuple-element.179), channel_id=1, source_target_pairs={{0,4},{4,8},{8,12},{12,16},{16,20},{20,24},{24,28},{1,5},{5,9},{9,... | collective-permute-start | bytes 49160 | tf_op jit(solution)/shard_map/ppermute | solution.py:21
  261.7 7.4 %collective-permute-start.55 = (f32[2,1,16,128]{3,2,1,0:T(8,128)S(1)}, f32[2,1,16,128]{3,2,1,0:T(8,128)S(1)}, u32[]{:S(2)}, u32[]{:S(2)}) collective-permute-start(f32[2,1,16,128]{3,2,1,0:T(8,128)S(1)} %get-tuple-element.176), channel_id=1, source_target_pairs={{4,0},{8,4},{12,8},{16,12},{20,16},{24,20},{28,24},{5,1},{9,5},{13... | collective-permute-start | bytes 49160 | tf_op jit(solution)/shard_map/ppermute | solution.py:24
  263.0 6.9 %collective-permute-start.56 = (f32[2,1,16,128]{3,2,1,0:T(8,128)S(1)}, f32[2,1,16,128]{3,2,1,0:T(8,128)S(1)}, u32[]{:S(2)}, u32[]{:S(2)}) collective-permute-start(f32[2,1,16,128]{3,2,1,0:T(8,128)S(1)} %get-tuple-element.175), channel_id=1, source_target_pairs={{0,4},{4,8},{8,12},{12,16},{16,20},{20,24},{24,28},{1,5},{5,9},{9,... | collective-permute-start | bytes 49160 | tf_op jit(solution)/shard_map/ppermute | solution.py:21
  278.8 7.4 %collective-permute-start.59 = (f32[2,1,16,128]{3,2,1,0:T(8,128)S(1)}, f32[2,1,16,128]{3,2,1,0:T(8,128)S(1)}, u32[]{:S(2)}, u32[]{:S(2)}) collective-permute-start(f32[2,1,16,128]{3,2,1,0:T(8,128)S(1)} %get-tuple-element.172), channel_id=1, source_target_pairs={{4,0},{8,4},{12,8},{16,12},{20,16},{24,20},{28,24},{5,1},{9,5},{13... | collective-permute-start | bytes 49160 | tf_op jit(solution)/shard_map/ppermute | solution.py:24
  280.1 6.9 %collective-permute-start.60 = (f32[2,1,16,128]{3,2,1,0:T(8,128)S(1)}, f32[2,1,16,128]{3,2,1,0:T(8,128)S(1)}, u32[]{:S(2)}, u32[]{:S(2)}) collective-permute-start(f32[2,1,16,128]{3,2,1,0:T(8,128)S(1)} %get-tuple-element.171), channel_id=1, source_target_pairs={{0,4},{4,8},{8,12},{12,16},{16,20},{20,24},{24,28},{1,5},{5,9},{9,... | collective-permute-start | bytes 49160 | tf_op jit(solution)/shard_map/ppermute | solution.py:21
  295.9 7.4 %collective-permute-start.63 = (f32[2,1,16,128]{3,2,1,0:T(8,128)S(1)}, f32[2,1,16,128]{3,2,1,0:T(8,128)S(1)}, u32[]{:S(2)}, u32[]{:S(2)}) collective-permute-start(f32[2,1,16,128]{3,2,1,0:T(8,128)S(1)} %get-tuple-element.168), channel_id=1, source_target_pairs={{4,0},{8,4},{12,8},{16,12},{20,16},{24,20},{28,24},{5,1},{9,5},{13... | collective-permute-start | bytes 49160 | tf_op jit(solution)/shard_map/ppermute | solution.py:24
  297.2 6.9 %collective-permute-start.64 = (f32[2,1,16,128]{3,2,1,0:T(8,128)S(1)}, f32[2,1,16,128]{3,2,1,0:T(8,128)S(1)}, u32[]{:S(2)}, u32[]{:S(2)}) collective-permute-start(f32[2,1,16,128]{3,2,1,0:T(8,128)S(1)} %get-tuple-element.167), channel_id=1, source_target_pairs={{0,4},{4,8},{8,12},{12,16},{16,20},{20,24},{24,28},{1,5},{5,9},{9,... | collective-permute-start | bytes 49160 | tf_op jit(solution)/shard_map/ppermute | solution.py:21
  313.0 7.4 %collective-permute-start.67 = (f32[2,1,16,128]{3,2,1,0:T(8,128)S(1)}, f32[2,1,16,128]{3,2,1,0:T(8,128)S(1)}, u32[]{:S(2)}, u32[]{:S(2)}) collective-permute-start(f32[2,1,16,128]{3,2,1,0:T(8,128)S(1)} %get-tuple-element.164), channel_id=1, source_target_pairs={{4,0},{8,4},{12,8},{16,12},{20,16},{24,20},{28,24},{5,1},{9,5},{13... | collective-permute-start | bytes 49160 | tf_op jit(solution)/shard_map/ppermute | solution.py:24
  314.3 6.9 %collective-permute-start.68 = (f32[2,1,16,128]{3,2,1,0:T(8,128)S(1)}, f32[2,1,16,128]{3,2,1,0:T(8,128)S(1)}, u32[]{:S(2)}, u32[]{:S(2)}) collective-permute-start(f32[2,1,16,128]{3,2,1,0:T(8,128)S(1)} %get-tuple-element.163), channel_id=1, source_target_pairs={{0,4},{4,8},{8,12},{12,16},{16,20},{20,24},{24,28},{1,5},{5,9},{9,... | collective-permute-start | bytes 49160 | tf_op jit(solution)/shard_map/ppermute | solution.py:21
  330.1 7.4 %collective-permute-start.71 = (f32[2,1,16,128]{3,2,1,0:T(8,128)S(1)}, f32[2,1,16,128]{3,2,1,0:T(8,128)S(1)}, u32[]{:S(2)}, u32[]{:S(2)}) collective-permute-start(f32[2,1,16,128]{3,2,1,0:T(8,128)S(1)} %get-tuple-element.160), channel_id=1, source_target_pairs={{4,0},{8,4},{12,8},{16,12},{20,16},{24,20},{28,24},{5,1},{9,5},{13... | collective-permute-start | bytes 49160 | tf_op jit(solution)/shard_map/ppermute | solution.py:24
  331.4 6.9 %collective-permute-start.72 = (f32[2,1,16,128]{3,2,1,0:T(8,128)S(1)}, f32[2,1,16,128]{3,2,1,0:T(8,128)S(1)}, u32[]{:S(2)}, u32[]{:S(2)}) collective-permute-start(f32[2,1,16,128]{3,2,1,0:T(8,128)S(1)} %get-tuple-element.159), channel_id=1, source_target_pairs={{0,4},{4,8},{8,12},{12,16},{16,20},{20,24},{24,28},{1,5},{5,9},{9,... | collective-permute-start | bytes 49160 | tf_op jit(solution)/shard_map/ppermute | solution.py:21
  346.1 7.4 %collective-permute-start.75 = (f32[2,1,16,128]{3,2,1,0:T(8,128)S(1)}, f32[2,1,16,128]{3,2,1,0:T(8,128)S(1)}, u32[]{:S(2)}, u32[]{:S(2)}) collective-permute-start(f32[2,1,16,128]{3,2,1,0:T(8,128)S(1)} %get-tuple-element.156), channel_id=1, source_target_pairs={{4,0},{8,4},{12,8},{16,12},{20,16},{24,20},{28,24},{5,1},{9,5},{13... | collective-permute-start | bytes 49160 | tf_op jit(solution)/shard_map/ppermute | solution.py:24
  347.4 6.9 %collective-permute-start.76 = (f32[2,1,16,128]{3,2,1,0:T(8,128)S(1)}, f32[2,1,16,128]{3,2,1,0:T(8,128)S(1)}, u32[]{:S(2)}, u32[]{:S(2)}) collective-permute-start(f32[2,1,16,128]{3,2,1,0:T(8,128)S(1)} %get-tuple-element.155), channel_id=1, source_target_pairs={{0,4},{4,8},{8,12},{12,16},{16,20},{20,24},{24,28},{1,5},{5,9},{9,... | collective-permute-start | bytes 49160 | tf_op jit(solution)/shard_map/ppermute | solution.py:21
  362.0 8.1 %collective-permute-start.79 = (f32[2,1,16,128]{3,2,1,0:T(8,128)S(1)}, f32[2,1,16,128]{3,2,1,0:T(8,128)S(1)}, u32[]{:S(2)}, u32[]{:S(2)}) collective-permute-start(f32[2,1,16,128]{3,2,1,0:T(8,128)S(1)} %get-tuple-element.152), channel_id=1, source_target_pairs={{4,0},{8,4},{12,8},{16,12},{20,16},{24,20},{28,24},{5,1},{9,5},{13... | collective-permute-start | bytes 49160 | tf_op jit(solution)/shard_map/ppermute | solution.py:24
  363.3 6.9 %collective-permute-start.80 = (f32[2,1,16,128]{3,2,1,0:T(8,128)S(1)}, f32[2,1,16,128]{3,2,1,0:T(8,128)S(1)}, u32[]{:S(2)}, u32[]{:S(2)}) collective-permute-start(f32[2,1,16,128]{3,2,1,0:T(8,128)S(1)} %get-tuple-element.151), channel_id=1, source_target_pairs={{0,4},{4,8},{8,12},{12,16},{16,20},{20,24},{24,28},{1,5},{5,9},{9,... | collective-permute-start | bytes 49160 | tf_op jit(solution)/shard_map/ppermute | solution.py:21
  379.1 16.2 %collective-permute-start.83 = (f32[2,1,16,128]{3,2,1,0:T(8,128)}, f32[2,1,16,128]{3,2,1,0:T(8,128)S(1)}, u32[]{:S(2)}, u32[]{:S(2)}) collective-permute-start(f32[2,1,16,128]{3,2,1,0:T(8,128)} %get-tuple-element.148), channel_id=1, source_target_pairs={{4,0},{8,4},{12,8},{16,12},{20,16},{24,20},{28,24},{5,1},{9,5},{13... | collective-permute-start | bytes 49160 | tf_op jit(solution)/shard_map/ppermute | solution.py:24
  380.6 14.7 %collective-permute-start.84 = (f32[2,1,16,128]{3,2,1,0:T(8,128)}, f32[2,1,16,128]{3,2,1,0:T(8,128)}, u32[]{:S(2)}, u32[]{:S(2)}) collective-permute-start(f32[2,1,16,128]{3,2,1,0:T(8,128)} %get-tuple-element.147), channel_id=1, source_target_pairs={{0,4},{4,8},{8,12},{12,16},{16,20},{20,24},{24,28},{1,5},{5,9},{9,... | collective-permute-start | bytes 49160 | tf_op jit(solution)/shard_map/ppermute | solution.py:21
  396.3 7.1 %collective-permute-start.85 = (f32[2,18,1,128]{3,2,1,0:T(1,128)S(1)}, f32[2,18,1,128]{3,2,1,0:T(1,128)S(1)}, u32[]{:S(2)}, u32[]{:S(2)}) collective-permute-start(f32[2,18,1,128]{3,2,1,0:T(1,128)S(1)} %get-tuple-element.89), channel_id=1, source_target_pairs={{1,0},{2,1},{3,2},{5,4},{6,5},{7,6},{9,8},{10,9},{11,10},{13,12},{... | collective-permute-start | bytes 55304 | tf_op jit(solution)/shard_map/ppermute | solution.py:24
  407.9 25.6 %collective-permute-start.87 = (f32[2,1,16,128]{3,2,1,0:T(8,128)}, f32[2,1,16,128]{3,2,1,0:T(8,128)S(1)}, u32[]{:S(2)}, u32[]{:S(2)}) collective-permute-start(f32[2,1,16,128]{3,2,1,0:T(8,128)} %get-tuple-element.144), channel_id=1, source_target_pairs={{4,0},{8,4},{12,8},{16,12},{20,16},{24,20},{28,24},{5,1},{9,5},{13... | collective-permute-start | bytes 49160 | tf_op jit(solution)/shard_map/ppermute | solution.py:24
  409.2 24.3 %collective-permute-start.88 = (f32[2,1,16,128]{3,2,1,0:T(8,128)}, f32[2,1,16,128]{3,2,1,0:T(8,128)}, u32[]{:S(2)}, u32[]{:S(2)}) collective-permute-start(f32[2,1,16,128]{3,2,1,0:T(8,128)} %get-tuple-element.143), channel_id=1, source_target_pairs={{0,4},{4,8},{8,12},{12,16},{16,20},{20,24},{24,28},{1,5},{5,9},{9,... | collective-permute-start | bytes 49160 | tf_op jit(solution)/shard_map/ppermute | solution.py:21
  434.5 7.1 %collective-permute-start.89 = (f32[2,18,1,128]{3,2,1,0:T(1,128)S(1)}, f32[2,18,1,128]{3,2,1,0:T(1,128)S(1)}, u32[]{:S(2)}, u32[]{:S(2)}) collective-permute-start(f32[2,18,1,128]{3,2,1,0:T(1,128)S(1)} %get-tuple-element.87), channel_id=1, source_target_pairs={{1,0},{2,1},{3,2},{5,4},{6,5},{7,6},{9,8},{10,9},{11,10},{13,12},{... | collective-permute-start | bytes 55304 | tf_op jit(solution)/shard_map/ppermute | solution.py:24
  444.7 8.4 %collective-permute-start.91 = (f32[2,1,16,128]{3,2,1,0:T(8,128)S(1)}, f32[2,1,16,128]{3,2,1,0:T(8,128)S(1)}, u32[]{:S(2)}, u32[]{:S(2)}) collective-permute-start(f32[2,1,16,128]{3,2,1,0:T(8,128)S(1)} %get-tuple-element.140), channel_id=1, source_target_pairs={{4,0},{8,4},{12,8},{16,12},{20,16},{24,20},{28,24},{5,1},{9,5},{13... | collective-permute-start | bytes 49160 | tf_op jit(solution)/shard_map/ppermute | solution.py:24
  446.0 7.1 %collective-permute-start.92 = (f32[2,1,16,128]{3,2,1,0:T(8,128)S(1)}, f32[2,1,16,128]{3,2,1,0:T(8,128)S(1)}, u32[]{:S(2)}, u32[]{:S(2)}) collective-permute-start(f32[2,1,16,128]{3,2,1,0:T(8,128)S(1)} %get-tuple-element.139), channel_id=1, source_target_pairs={{0,4},{4,8},{8,12},{12,16},{16,20},{20,24},{24,28},{1,5},{5,9},{9,... | collective-permute-start | bytes 49160 | tf_op jit(solution)/shard_map/ppermute | solution.py:21
  463.0 25.8 %collective-permute-start.95 = (f32[2,1,16,128]{3,2,1,0:T(8,128)}, f32[2,1,16,128]{3,2,1,0:T(8,128)S(1)}, u32[]{:S(2)}, u32[]{:S(2)}) collective-permute-start(f32[2,1,16,128]{3,2,1,0:T(8,128)} %get-tuple-element.136), channel_id=1, source_target_pairs={{4,0},{8,4},{12,8},{16,12},{20,16},{24,20},{28,24},{5,1},{9,5},{13... | collective-permute-start | bytes 49160 | tf_op jit(solution)/shard_map/ppermute | solution.py:24
  464.3 24.5 %collective-permute-start.96 = (f32[2,1,16,128]{3,2,1,0:T(8,128)}, f32[2,1,16,128]{3,2,1,0:T(8,128)}, u32[]{:S(2)}, u32[]{:S(2)}) collective-permute-start(f32[2,1,16,128]{3,2,1,0:T(8,128)} %get-tuple-element.135), channel_id=1, source_target_pairs={{0,4},{4,8},{8,12},{12,16},{16,20},{20,24},{24,28},{1,5},{5,9},{9,... | collective-permute-start | bytes 49160 | tf_op jit(solution)/shard_map/ppermute | solution.py:21
  489.8 7.1 %collective-permute-start.97 = (f32[2,18,1,128]{3,2,1,0:T(1,128)S(1)}, f32[2,18,1,128]{3,2,1,0:T(1,128)S(1)}, u32[]{:S(2)}, u32[]{:S(2)}) collective-permute-start(f32[2,18,1,128]{3,2,1,0:T(1,128)S(1)} %get-tuple-element.83), channel_id=1, source_target_pairs={{1,0},{2,1},{3,2},{5,4},{6,5},{7,6},{9,8},{10,9},{11,10},{13,12},{... | collective-permute-start | bytes 55304 | tf_op jit(solution)/shard_map/ppermute | solution.py:24
  500.2 6.3 %collective-permute-start.100 = (f32[2,1,16,128]{3,2,1,0:T(8,128)S(1)}, f32[2,1,16,128]{3,2,1,0:T(8,128)S(1)}, u32[]{:S(2)}, u32[]{:S(2)}) collective-permute-start(f32[2,1,16,128]{3,2,1,0:T(8,128)S(1)} %get-tuple-element.131), channel_id=1, source_target_pairs={{0,4},{4,8},{8,12},{12,16},{16,20},{20,24},{24,28},{1,5},{5,9},{9,... | collective-permute-start | bytes 49160 | tf_op jit(solution)/shard_map/ppermute | solution.py:21
  508.3 6.3 %collective-permute-start.101 = (f32[2,18,1,128]{3,2,1,0:T(1,128)S(1)}, f32[2,18,1,128]{3,2,1,0:T(1,128)S(1)}, u32[]{:S(2)}, u32[]{:S(2)}) collective-permute-start(f32[2,18,1,128]{3,2,1,0:T(1,128)S(1)} %get-tuple-element.81), channel_id=1, source_target_pairs={{1,0},{2,1},{3,2},{5,4},{6,5},{7,6},{9,8},{10,9},{11,10},{13,12},{... | collective-permute-start | bytes 55304 | tf_op jit(solution)/shard_map/ppermute | solution.py:24
  509.6 6.3 %collective-permute-start.102 = (f32[2,18,1,128]{3,2,1,0:T(1,128)S(1)}, f32[2,18,1,128]{3,2,1,0:T(1,128)S(1)}, u32[]{:S(2)}, u32[]{:S(2)}) collective-permute-start(f32[2,18,1,128]{3,2,1,0:T(1,128)S(1)} %get-tuple-element.82), channel_id=1, source_target_pairs={{0,1},{1,2},{2,3},{4,5},{5,6},{6,7},{8,9},{9,10},{10,11},{12,13},{... | collective-permute-start | bytes 55304 | tf_op jit(solution)/shard_map/ppermute | solution.py:21
  (99 other events, 1850.6 us)
